TPU v7x, 32 devices: a whole 2x2x4 slice. The times are simulated.
32 devices in a mesh: dp: 4 (over y, x), tensor: 8 (over z, core).
Axes of the slice: x: 2, y: 2, z: 4, core: 2. Of those that a mesh axis runs over, the one named last changes fastest.
Arguments:
- latents: bfloat16 [4, 2048, 1152], P('dp', 'tensor'), may hold values from -6 to 6
- conditioning: bfloat16 [4, 1152], P('dp', 'tensor'), may hold values from -6 to 6
- ada_weight: bfloat16 [2, 1152, 6912], P(None, 'tensor'), may hold values from -0.1875 to 0.1875
- ada_bias: bfloat16 [2, 6912], replicated, may hold values from -3 to 3
- qkv_weight: bfloat16 [2, 1152, 3, 1152], P(None, None, None, 'tensor'), may hold values from -0.1875 to 0.1875
- qkv_bias: bfloat16 [2, 2, 1152], P(None, None, 'tensor'), may hold values from -3 to 3
- out_weight: bfloat16 [2, 1152, 1152], P(None, 'tensor'), may hold values from -0.75 to 0.75
- out_bias: bfloat16 [2, 1152], replicated, may hold values from -3 to 3
- fc1_weight: bfloat16 [2, 1152, 4608], P(None, None, 'tensor'), may hold values from -0.1875 to 0.1875
- fc1_bias: bfloat16 [2, 4608], P(None, 'tensor'), may hold values from -3 to 3
- fc2_weight: bfloat16 [2, 4608, 1152], P(None, 'tensor'), may hold values from -0.09375 to 0.09375
- fc2_bias: bfloat16 [2, 1152], replicated, may hold values from -3 to 3
- out_grad: bfloat16 [4, 2048, 1152], P('dp', 'tensor'), may hold values from -6 to 6
Outputs:
- layer_output: bfloat16 [4, 2048, 1152], P('dp', 'tensor')
- latents_grad: bfloat16 [4, 2048, 1152], P('dp', 'tensor')
- conditioning_grad: bfloat16 [4, 1152], P('dp', 'tensor')
- ada_weight_grad: float32 [2, 1152, 6912], P(None, 'tensor')
- ada_bias_grad: float32 [2, 6912], replicated
- qkv_weight_grad: float32 [2, 1152, 3, 1152], P(None, None, None, 'tensor')
- qkv_bias_grad: float32 [2, 2, 1152], P(None, None, 'tensor')
- out_weight_grad: float32 [2, 1152, 1152], P(None, 'tensor')
- out_bias_grad: float32 [2, 1152], replicated
- fc1_weight_grad: float32 [2, 1152, 4608], P(None, None, 'tensor')
- fc1_bias_grad: float32 [2, 4608], P(None, 'tensor')
- fc2_weight_grad: float32 [2, 4608, 1152], P(None, 'tensor')
- fc2_bias_grad: float32 [2, 1152], replicated
All inputs are finite; a program needn't handle non-finite values.
Results may differ from a plain program's by a relative error of at most 0.04.
Values may be sent and summed in bfloat16 or wider, within the bound.
A program may use at most 256 MiB of HBM per device.

v0:
```python
from functools import partial
import jax
import jax.numpy as jnp
from jax import lax
from jax.sharding import PartitionSpec as P

HEAD_DIM = 72
PATCHES = 256
FRAMES = 8
LAYERS = 2


def normalize(stream):
    centered = stream - jnp.mean(stream, axis=-1, keepdims=True)
    variance = jnp.mean(centered * centered, axis=-1, keepdims=True)
    return centered * lax.rsqrt(variance + 1e-06)


def modulate(stream, shift_in, scale_in):
    return normalize(stream) * (1.0 + scale_in) + shift_in


def grouped(token_rows, spatial):
    heads_here = token_rows.shape[1] // HEAD_DIM
    shaped = token_rows.reshape(FRAMES, PATCHES, heads_here, HEAD_DIM)
    if spatial:
        return shaped
    return jnp.transpose(shaped, (1, 0, 2, 3))


def ungrouped(groups, spatial):
    if not spatial:
        groups = jnp.transpose(groups, (1, 0, 2, 3))
    return groups.reshape(FRAMES * PATCHES, groups.shape[2] * HEAD_DIM)


def softmax_rows(query_g, key_g):
    scores = jnp.einsum(
        "gqhd,gkhd->ghqk", query_g, key_g, preferred_element_type=jnp.float32
    ) * HEAD_DIM ** (-0.5)
    return jax.nn.softmax(scores, axis=-1)


def attend(query_rows, key_rows, value_rows, spatial):
    attn_probs = softmax_rows(grouped(query_rows, spatial), grouped(key_rows, spatial)).astype(
        jnp.bfloat16
    )
    mixed = jnp.einsum(
        "ghqk,gkhd->gqhd",
        attn_probs,
        grouped(value_rows, spatial),
        preferred_element_type=jnp.float32,
    )
    return ungrouped(mixed, spatial)


def attend_back(query_rows, key_rows, value_rows, mixed_grad, spatial):
    query_g = grouped(query_rows, spatial)
    key_g = grouped(key_rows, spatial)
    value_g = grouped(value_rows, spatial)
    grad_g = grouped(mixed_grad, spatial)
    probs_full = softmax_rows(query_g, key_g)
    value_grad = jnp.einsum(
        "ghqk,gqhd->gkhd",
        probs_full.astype(jnp.bfloat16),
        grad_g,
        preferred_element_type=jnp.float32,
    )
    probs_grad = jnp.einsum("gqhd,gkhd->ghqk", grad_g, value_g, preferred_element_type=jnp.float32)
    score_grad = probs_full * (
        probs_grad - jnp.sum(probs_grad * probs_full, axis=-1, keepdims=True)
    )
    score_low = score_grad.astype(jnp.bfloat16)
    factor = HEAD_DIM ** (-0.5)
    query_grad = (
        jnp.einsum("ghqk,gkhd->gqhd", score_low, key_g, preferred_element_type=jnp.float32) * factor
    )
    key_grad = (
        jnp.einsum("ghqk,gqhd->gkhd", score_low, query_g, preferred_element_type=jnp.float32)
        * factor
    )
    return (
        ungrouped(query_grad, spatial),
        ungrouped(key_grad, spatial),
        ungrouped(value_grad, spatial),
    )


def spread_rows(row_block):
    return lax.all_gather(row_block, "tensor", axis=0, tiled=True)


def reduce_rows(partial_terms):
    return lax.psum_scatter(
        partial_terms.astype(jnp.bfloat16), "tensor", scatter_dimension=0, tiled=True
    ).astype(jnp.float32)


def spread_grads(row_block):
    return lax.all_gather(row_block, "tensor", axis=0, tiled=True)


def reduce_grads(partial_terms):
    return lax.psum_scatter(
        partial_terms.astype(jnp.bfloat16), "tensor", scatter_dimension=0, tiled=True
    ).astype(jnp.float32)


def layer_forward(stream, modulation, params, spatial):
    qkv_w, qkv_b, out_w, out_b, fc1_w, fc1_b, fc2_w, fc2_b = params
    shift_att, scale_att, gate_att, shift_mlp, scale_mlp, gate_mlp = jnp.split(modulation, 6)
    normed = spread_rows(modulate(stream, shift_att, scale_att).astype(jnp.bfloat16))
    head_width = qkv_w.shape[2]
    projected = jnp.dot(
        normed, qkv_w.reshape(qkv_w.shape[0], 3 * head_width), preferred_element_type=jnp.float32
    )
    query_rows = (projected[:, :head_width] + qkv_b[0].astype(jnp.float32)).astype(jnp.bfloat16)
    key_rows = projected[:, head_width : 2 * head_width].astype(jnp.bfloat16)
    value_rows = (projected[:, 2 * head_width :] + qkv_b[1].astype(jnp.float32)).astype(
        jnp.bfloat16
    )
    heads_out = attend(query_rows, key_rows, value_rows, spatial).astype(jnp.bfloat16)
    attn_branch = reduce_rows(
        jnp.dot(heads_out, out_w, preferred_element_type=jnp.float32)
    ) + out_b.astype(jnp.float32)
    middle = stream + gate_att * attn_branch
    normed_mlp = spread_rows(modulate(middle, shift_mlp, scale_mlp).astype(jnp.bfloat16))
    hidden = jnp.dot(normed_mlp, fc1_w, preferred_element_type=jnp.float32) + fc1_b.astype(
        jnp.float32
    )
    activated = jax.nn.gelu(hidden, approximate=True).astype(jnp.bfloat16)
    mlp_branch = reduce_rows(
        jnp.dot(activated, fc2_w, preferred_element_type=jnp.float32)
    ) + fc2_b.astype(jnp.float32)
    result = middle + gate_mlp * mlp_branch
    saved = (
        normed,
        query_rows,
        key_rows,
        value_rows,
        heads_out,
        attn_branch,
        middle,
        normed_mlp,
        hidden,
        mlp_branch,
    )
    return (result, saved)


def layer_backward(stream, modulation, params, saved, stream_grad, spatial):
    qkv_w, qkv_b, out_w, out_b, fc1_w, fc1_b, fc2_w, fc2_b = params
    (
        normed,
        query_rows,
        key_rows,
        value_rows,
        heads_out,
        attn_branch,
        middle,
        normed_mlp,
        hidden,
        mlp_branch,
    ) = saved
    shift_att, scale_att, gate_att, shift_mlp, scale_mlp, gate_mlp = jnp.split(modulation, 6)
    head_width = qkv_w.shape[2]
    mlp_grad = (gate_mlp * stream_grad).astype(jnp.bfloat16)
    gate_mlp_grad = jnp.sum(stream_grad * mlp_branch, axis=0)
    fc2_b_grad = jnp.sum(mlp_grad, axis=0, dtype=jnp.float32)
    mlp_grad_all = spread_grads(mlp_grad)
    gelu_out, gelu_back = jax.vjp(partial(jax.nn.gelu, approximate=True), hidden)
    activated = gelu_out.astype(jnp.bfloat16)
    fc2_w_grad = jnp.einsum(
        "tf,td->fd", activated, mlp_grad_all, preferred_element_type=jnp.float32
    )
    act_grad = jnp.einsum("td,fd->tf", mlp_grad_all, fc2_w, preferred_element_type=jnp.float32)
    hidden_grad = gelu_back(act_grad)[0].astype(jnp.bfloat16)
    fc1_b_grad = jnp.sum(hidden_grad, axis=0, dtype=jnp.float32)
    fc1_w_grad = jnp.einsum(
        "td,tf->df", normed_mlp, hidden_grad, preferred_element_type=jnp.float32
    )
    mlp_in_grad = reduce_grads(
        jnp.einsum("tf,df->td", hidden_grad, fc1_w, preferred_element_type=jnp.float32)
    )
    _, mlp_norm_back = jax.vjp(modulate, middle, shift_mlp, scale_mlp)
    middle_part, shift_mlp_grad, scale_mlp_grad = mlp_norm_back(mlp_in_grad)
    middle_grad = stream_grad + middle_part
    attn_grad = (gate_att * middle_grad).astype(jnp.bfloat16)
    gate_att_grad = jnp.sum(middle_grad * attn_branch, axis=0)
    out_b_grad = jnp.sum(attn_grad, axis=0, dtype=jnp.float32)
    attn_grad_all = spread_grads(attn_grad)
    out_w_grad = jnp.einsum(
        "tw,td->wd", heads_out, attn_grad_all, preferred_element_type=jnp.float32
    )
    heads_grad = jnp.einsum(
        "td,wd->tw", attn_grad_all, out_w, preferred_element_type=jnp.float32
    ).astype(jnp.bfloat16)
    query_grad, key_grad, value_grad = attend_back(
        query_rows, key_rows, value_rows, heads_grad, spatial
    )
    qkv_grad = jnp.concatenate([query_grad, key_grad, value_grad], axis=1).astype(jnp.bfloat16)
    qkv_b_grad = jnp.stack(
        [
            jnp.sum(qkv_grad[:, :head_width], axis=0, dtype=jnp.float32),
            jnp.sum(qkv_grad[:, 2 * head_width :], axis=0, dtype=jnp.float32),
        ]
    )
    qkv_flat = qkv_w.reshape(qkv_w.shape[0], 3 * head_width)
    qkv_w_grad = jnp.einsum(
        "td,tw->dw", normed, qkv_grad, preferred_element_type=jnp.float32
    ).reshape(qkv_w.shape)
    attn_in_grad = reduce_grads(
        jnp.einsum("tw,dw->td", qkv_grad, qkv_flat, preferred_element_type=jnp.float32)
    )
    _, att_norm_back = jax.vjp(modulate, stream, shift_att, scale_att)
    stream_part, shift_att_grad, scale_att_grad = att_norm_back(attn_in_grad)
    input_grad = middle_grad + stream_part
    modulation_grad = jnp.concatenate(
        [
            shift_att_grad,
            scale_att_grad,
            gate_att_grad,
            shift_mlp_grad,
            scale_mlp_grad,
            gate_mlp_grad,
        ]
    )
    return (
        input_grad,
        modulation_grad,
        (
            qkv_w_grad,
            qkv_b_grad,
            out_w_grad,
            out_b_grad,
            fc1_w_grad,
            fc1_b_grad,
            fc2_w_grad,
            fc2_b_grad,
        ),
    )


def per_device(
    latents,
    conditioning,
    ada_weight,
    ada_bias,
    qkv_weight,
    qkv_bias,
    out_weight,
    out_bias,
    fc1_weight,
    fc1_bias,
    fc2_weight,
    fc2_bias,
    out_grad,
):
    cond_row = conditioning[0].astype(jnp.float32)
    silu_out, silu_back = jax.vjp(jax.nn.silu, cond_row)
    silu_cond = silu_out.astype(jnp.bfloat16)
    ada_terms = jnp.einsum("d,ldm->lm", silu_cond, ada_weight, preferred_element_type=jnp.float32)
    modulations = lax.psum(ada_terms, "tensor") + ada_bias.astype(jnp.float32)
    stacked = (
        qkv_weight,
        qkv_bias,
        out_weight,
        out_bias,
        fc1_weight,
        fc1_bias,
        fc2_weight,
        fc2_bias,
    )
    stream = latents[0].astype(jnp.float32)
    inputs_kept = []
    saved_all = []
    for layer_idx in range(LAYERS):
        params = tuple((member[layer_idx] for member in stacked))
        inputs_kept.append(stream)
        stream, saved = layer_forward(stream, modulations[layer_idx], params, layer_idx % 2 == 0)
        saved_all.append(saved)
    layer_output = stream.astype(jnp.bfloat16)[None]
    stream_grad = out_grad[0].astype(jnp.float32)
    mod_grads = [None] * LAYERS
    layer_grads = [None] * LAYERS
    for layer_idx in reversed(range(LAYERS)):
        params = tuple((member[layer_idx] for member in stacked))
        spatial = layer_idx % 2 == 0
        saved = layer_forward(inputs_kept[layer_idx], modulations[layer_idx], params, spatial)[1]
        stream_grad, mod_grads[layer_idx], layer_grads[layer_idx] = layer_backward(
            inputs_kept[layer_idx], modulations[layer_idx], params, saved, stream_grad, spatial
        )

    def collect(position):
        return jnp.stack([member[position] for member in layer_grads])

    mod_sum, out_b_sum, fc2_b_sum = (
        lax.psum(jnp.stack(mod_grads).astype(jnp.bfloat16), "tensor").astype(jnp.float32),
        lax.psum(collect(3).astype(jnp.bfloat16), "tensor").astype(jnp.float32),
        lax.psum(collect(7).astype(jnp.bfloat16), "tensor").astype(jnp.float32),
    )
    mod_low = mod_sum.astype(jnp.bfloat16)
    ada_w_grad = (
        silu_cond.astype(jnp.float32)[None, :, None] * mod_low.astype(jnp.float32)[:, None, :]
    )
    ada_b_grad = mod_low.astype(jnp.float32)
    silu_grad = jnp.einsum("lm,ldm->d", mod_low, ada_weight, preferred_element_type=jnp.float32)
    cond_grad = silu_back(silu_grad)[0]
    summed = (
        lax.psum(ada_w_grad.astype(jnp.bfloat16), "dp").astype(jnp.float32),
        lax.psum(ada_b_grad.astype(jnp.bfloat16), "dp").astype(jnp.float32),
        lax.psum(collect(0).astype(jnp.bfloat16), "dp").astype(jnp.float32),
        lax.psum(collect(1).astype(jnp.bfloat16), "dp").astype(jnp.float32),
        lax.psum(collect(2).astype(jnp.bfloat16), "dp").astype(jnp.float32),
        lax.psum(out_b_sum.astype(jnp.bfloat16), "dp").astype(jnp.float32),
        lax.psum(collect(4).astype(jnp.bfloat16), "dp").astype(jnp.float32),
        lax.psum(collect(5).astype(jnp.bfloat16), "dp").astype(jnp.float32),
        lax.psum(collect(6).astype(jnp.bfloat16), "dp").astype(jnp.float32),
        lax.psum(fc2_b_sum.astype(jnp.bfloat16), "dp").astype(jnp.float32),
    )
    return (
        layer_output,
        stream_grad.astype(jnp.bfloat16)[None],
        cond_grad.astype(jnp.bfloat16)[None],
        summed[0],
        summed[1],
        summed[2],
        summed[3],
        summed[4],
        summed[5],
        summed[6],
        summed[7],
        summed[8],
        summed[9],
    )


def solution(mesh):
    in_specs = (
        P("dp", "tensor", None),
        P("dp", "tensor"),
        P(None, "tensor", None),
        P(),
        P(None, None, None, "tensor"),
        P(None, None, "tensor"),
        P(None, "tensor", None),
        P(),
        P(None, None, "tensor"),
        P(None, "tensor"),
        P(None, "tensor", None),
        P(),
        P("dp", "tensor", None),
    )
    out_specs = (
        P("dp", "tensor", None),
        P("dp", "tensor", None),
        P("dp", "tensor"),
        P(None, "tensor", None),
        P(),
        P(None, None, None, "tensor"),
        P(None, None, "tensor"),
        P(None, "tensor", None),
        P(),
        P(None, None, "tensor"),
        P(None, "tensor"),
        P(None, "tensor", None),
        P(),
    )
    return jax.shard_map(
        per_device, mesh=mesh, in_specs=in_specs, out_specs=out_specs, check_vma=False
    )
```

profile of v0, /device:TPU:0, one launch (start us, length us, event | category | flops | bytes accessed | tf_op | source)
XLA Modules:
  0.0 1360.1 jit_solution(16830422912774858308)
XLA Ops:
  11.1 2.8 fusion.180
  14.0 30.9 %psum.98 = f32[2,6912]{1,0:T(2,128)S(1)} all-reduce(f32[2,6912]{1,0:T(2,128)S(1)} %bitcast.362), channel_id=1, replica_groups=mesh['dp'=4,'tensor'=8] {'tensor'}, use_global_device_ids=true, to_apply=%region_0.1 | all-reduce | flops 13824 | bytes 110592 | tf_op jit(solution)/shard_map/psum | solution.py:263
  48.3 48.6 %all-gather.9.cloned.1.call-done = bf16[2048,1152]{1,0:T(8,128)(2,1)} async-done(((bf16[256,1152]{1,0:T(8,128)(2,1)}), bf16[2048,1152]{1,0:T(8,128)(2,1)}) %all-gather.9.cloned.1.call-update) | async-done | bytes 4718608 | tf_op jit(solution)/shard_map/all_gather | solution.py:90
  96.8 5.1 fusion.181
  104.4 3.2 fusion.168
  110.7 3.8 convolution_convert_fusion.7
  115.8 52.6 %reduce-scatter.9.cloned.1.call-done = bf16[256,1152]{1,0:T(8,128)(2,1)} async-done(((bf16[2048,1152]{1,0:T(8,128)(2,1)}), bf16[256,1152]{1,0:T(8,128)(2,1)}) %reduce-scatter.9.cloned.1.call-update) | async-done | bytes 589840 | tf_op jit(solution)/shard_map/reduce_scatter | solution.py:94
  173.6 49.3 %all-gather.11.cloned.1.call-done = bf16[2048,1152]{1,0:T(8,128)(2,1)} async-done(((bf16[256,1152]{1,0:T(8,128)(2,1)}), bf16[2048,1152]{1,0:T(8,128)(2,1)}) %all-gather.11.cloned.1.call-update) | async-done | bytes 4718608 | tf_op jit(solution)/shard_map/all_gather | solution.py:90
  223.0 5.6 fusion.59
  228.7 2.2 copy-done.121
  230.9 6.7 convolution_convert_fusion.6
  238.9 52.6 %reduce-scatter.11.cloned.1.call-done = bf16[256,1152]{1,0:T(8,128)(2,1)} async-done(((bf16[2048,1152]{1,0:T(8,128)(2,1)}), bf16[256,1152]{1,0:T(8,128)(2,1)}) %reduce-scatter.11.cloned.1.call-update) | async-done | bytes 589840 | tf_op jit(solution)/shard_map/reduce_scatter | solution.py:94
  294.5 50.2 %all-gather.13.cloned.1.call-done = bf16[2048,1152]{1,0:T(8,128)(2,1)} async-done(((bf16[256,1152]{1,0:T(8,128)(2,1)}), bf16[2048,1152]{1,0:T(8,128)(2,1)}) %all-gather.13.cloned.1.call-update) | async-done | bytes 4718608 | tf_op jit(solution)/shard_map/all_gather | solution.py:90
  344.7 4.8 fusion.182
  356.7 5.3 fusion.169
  362.0 3.7 fusion.40
  368.6 4.8 convolution_convert_fusion.5
  373.4 53.9 %reduce-scatter.13.cloned.1.call-done = bf16[256,1152]{1,0:T(8,128)(2,1)} async-done(((bf16[2048,1152]{1,0:T(8,128)(2,1)}), bf16[256,1152]{1,0:T(8,128)(2,1)}) %reduce-scatter.13.cloned.1.call-update) | async-done | bytes 589840 | tf_op jit(solution)/shard_map/reduce_scatter | solution.py:94
  431.9 2.6 fusion.159
  435.0 47.1 %all-gather.15.cloned.1.call-done = bf16[2048,1152]{1,0:T(8,128)(2,1)} async-done(((bf16[256,1152]{1,0:T(8,128)(2,1)}), bf16[2048,1152]{1,0:T(8,128)(2,1)}) %all-gather.15.cloned.1.call-update) | async-done | bytes 4718608 | tf_op jit(solution)/shard_map/all_gather | solution.py:90
  482.1 8.2 fusion.51
  490.2 44.6 %all-gather.17.cloned.1.call-done = bf16[2048,1152]{1,0:T(8,128)(2,1)} async-done(((bf16[256,1152]{1,0:T(8,128)(2,1)}), bf16[2048,1152]{1,0:T(8,128)(2,1)}) %all-gather.17.cloned.1.call-update) | async-done | bytes 4718608 | tf_op jit(solution)/shard_map/all_gather | solution.py:100
  534.8 9.9 fusion.178
  546.2 5.8 convolution_convert_fusion.3
  552.2 10.0 convolution_convert_fusion.4
  562.3 43.6 %reduce-scatter.17.cloned.1.call-done = bf16[256,1152]{1,0:T(8,128)(2,1)} async-done(((bf16[2048,1152]{1,0:T(8,128)(2,1)}), bf16[256,1152]{1,0:T(8,128)(2,1)}) %reduce-scatter.17.cloned.1.call-update) | async-done | bytes 589840 | tf_op jit(solution)/shard_map/reduce_scatter | solution.py:104
  605.9 2.1 fusion.74
  609.3 52.7 %reduce-scatter.15.cloned.1.call-done = bf16[256,1152]{1,0:T(8,128)(2,1)} async-done(((bf16[2048,1152]{1,0:T(8,128)(2,1)}), bf16[256,1152]{1,0:T(8,128)(2,1)}) %reduce-scatter.15.cloned.1.call-update) | async-done | bytes 589840 | tf_op jit(solution)/shard_map/reduce_scatter | solution.py:94
  662.0 2.7 fusion.164
  667.7 50.0 %all-gather.19.cloned.1.call-done = bf16[2048,1152]{1,0:T(8,128)(2,1)} async-done(((bf16[256,1152]{1,0:T(8,128)(2,1)}), bf16[2048,1152]{1,0:T(8,128)(2,1)}) %all-gather.19.cloned.1.call-update) | async-done | bytes 4718608 | tf_op jit(solution)/shard_map/all_gather | solution.py:100
  717.7 4.0 convolution_convert_fusion.17
  723.7 4.3 fusion.174
  731.7 2.3 fusion.175
  744.6 4.6 convolution_convert_fusion.1
  749.3 53.9 %reduce-scatter.19.cloned.1.call-done = bf16[256,1152]{1,0:T(8,128)(2,1)} async-done(((bf16[2048,1152]{1,0:T(8,128)(2,1)}), bf16[256,1152]{1,0:T(8,128)(2,1)}) %reduce-scatter.19.cloned.1.call-update) | async-done | bytes 589840 | tf_op jit(solution)/shard_map/reduce_scatter | solution.py:104
  805.2 2.2 fusion.75
  807.6 2.5 fusion.158
  810.4 49.9 %all-gather.21.cloned.1.call-done = bf16[2048,1152]{1,0:T(8,128)(2,1)} async-done(((bf16[256,1152]{1,0:T(8,128)(2,1)}), bf16[2048,1152]{1,0:T(8,128)(2,1)}) %all-gather.21.cloned.1.call-update) | async-done | bytes 4718608 | tf_op jit(solution)/shard_map/all_gather | solution.py:100
  860.3 9.9 fusion.179
  871.6 5.8 convolution_convert_fusion.2
  877.5 53.9 %reduce-scatter.21.cloned.1.call-done = bf16[256,1152]{1,0:T(8,128)(2,1)} async-done(((bf16[2048,1152]{1,0:T(8,128)(2,1)}), bf16[256,1152]{1,0:T(8,128)(2,1)}) %reduce-scatter.21.cloned.1.call-update) | async-done | bytes 589840 | tf_op jit(solution)/shard_map/reduce_scatter | solution.py:104
  931.4 2.4 fusion.76
  937.0 49.7 %all-gather.23.cloned.1.call-done = bf16[2048,1152]{1,0:T(8,128)(2,1)} async-done(((bf16[256,1152]{1,0:T(8,128)(2,1)}), bf16[2048,1152]{1,0:T(8,128)(2,1)}) %all-gather.23.cloned.1.call-update) | async-done | bytes 4718608 | tf_op jit(solution)/shard_map/all_gather | solution.py:100
  986.8 4.1 convolution_convert_fusion.16
  999.2 4.6 convolution_convert_fusion
  1005.0 7.3 fusion.22
  1012.4 9.2 fusion.20
  1024.0 2.6 fusion.79
  1026.6 3.5 fusion.24
  1030.2 5.9 convolution_convert_fusion.12
  1038.2 6.4 fusion.21
  1046.4 8.2 fusion.19
  1056.7 3.5 fusion.23
  1061.1 4.9 convolution_convert_fusion.13
  1074.2 26.9 %all-reduce = (bf16[2,6912]{1,0:T(2,128)(2,1)S(1)}, bf16[2,1152]{1,0:T(2,128)(2,1)S(1)}, bf16[2,1152]{1,0:T(2,128)(2,1)S(1)}) all-reduce(bf16[2,6912]{1,0:T(2,128)(2,1)S(1)} %pad_maximum_fusion.4, bf16[2,1152]{1,0:T(2,128)(2,1)S(1)} %get-tuple-element.108, ...), channel_id=1, replica_groups=mesh['dp'=4,'tensor'=8] {'tensor'}, use_global_device_ids=true, to_apply=%region_43.44 | all-reduce | flops 18432 | bytes 73728 | tf_op jit(solution)/shard_map/psum | solution.py:298
  1101.1 2.5 multiply_convert_fusion
  1104.6 3.2 fusion.128
  1108.5 18.3 %all-reduce.1 = (bf16[2,6912]{1,0:T(2,128)(2,1)S(1)}, bf16[2,2,144]{2,1,0:T(2,128)(2,1)S(1)}, bf16[2,1152]{1,0:T(2,128)(2,1)S(1)}, bf16[2,576]{1,0:T(2,128)(2,1)S(1)}, bf16[2,1152]{1,0:T(2,128)(2,1)S(1)}) all-reduce(bf16[2,6912]{1,0:T(2,128)(2,1)S(1)} %get-tuple-element.41, ...), channel_id=1, replica_groups=mesh['dp'=4,'tensor'=8] {'dp'}, use_global_device_ids=true, to_apply=%region_45.46 | all-reduce | flops 20160 | bytes 80640 | tf_op jit(solution)/shard_map/psum | solution.py:311
  1129.9 206.3 %all-reduce.5.cloned.1.call-done = (bf16[2,144,6912]{2,1,0:T(8,128)(2,1)}, bf16[2,1152,3,144]{1,3,2,0:T(8,128)(2,1)}, bf16[2,144,1152]{2,1,0:T(8,128)(2,1)}, bf1...) async-done(((bf16[2,144,6912]{2,1,0:T(8,128)(2,1)}, bf16[2,1152,3,144]{1,3,2,0:T(8,128)(2,1)}, bf16[2,144,1152]{2,1,0:T(8,128)(2,1)}, bf16[2,1152,576]{1,2,0:T(8,128)(2,1)}, ...) | async-done | bytes 11943952 | tf_op jit(solution)/shard_map/psum | solution.py:310
  1336.2 2.2 convert_element_type.435
  1338.4 6.0 convert_element_type.427
  1344.5 2.2 convert_element_type.429
  1347.5 2.7 convert_element_type.439
  1350.4 2.7 convert_element_type.443
  (423 shorter events, 100.0 us)
Async XLA Ops:
  7.2 89.7 %all-gather.9.cloned.1.call-start = ((), (), s32[]{:S(2)}) async-start(), calls=%async_computation.8 | async-start | bytes 5308416 | tf_op jit(solution)/shard_map/all_gather | solution.py:90
  7.9 6.0 copy-start.105
  9.1 36.5 %copy-start.66 = (f32[256]{0:T(256)}, f32[256]{0:T(256)S(1)}, u32[]{:S(2)}) copy-start(f32[256]{0:T(256)S(1)} %broadcast_multiply_fusion.3) | copy-start | bytes 3076
  10.5 35.1 %copy-start.78 = (f32[256]{0:T(256)}, f32[256]{0:T(256)S(1)}, u32[]{:S(2)}) copy-start(f32[256]{0:T(256)S(1)} %fusion.137) | copy-start | bytes 3076
  11.1 33.7 %copy-start.68 = (bf16[2,6912]{1,0:T(2,128)(2,1)S(1)}, bf16[2,6912]{1,0:T(2,128)(2,1)}, u32[]{:S(2)}) copy-start(bf16[2,6912]{1,0:T(2,128)(2,1)} %param.16) | copy-start | bytes 82948
  11.1 34.5 %copy-start = (bf16[1,256,1152]{2,1,0:T(8,128)(2,1)S(1)}, bf16[1,256,1152]{2,1,0:T(8,128)(2,1)}, u32[]{:S(2)}) copy-start(bf16[1,256,1152]{2,1,0:T(8,128)(2,1)} %param.13) | copy-start | bytes 1769476
  13.9 32.9 %copy-start.107 = (bf16[2,2,144]{2,1,0:T(2,128)(2,1)S(1)}, bf16[2,2,144]{2,1,0:T(2,128)(2,1)}, u32[]{:S(2)}) copy-start(bf16[2,2,144]{2,1,0:T(2,128)(2,1)} %param.18) | copy-start | bytes 3460
  13.9 32.9 %copy-start.30 = (bf16[2,1152,3,144]{1,3,2,0:T(8,128)(2,1)S(1)}, bf16[2,1152,3,144]{1,3,2,0:T(8,128)(2,1)}, u32[]{:S(2)}) copy-start(bf16[2,1152,3,144]{1,3,2,0:T(8,128)(2,1)} %param.17) | copy-start | bytes 5971972
  45.6 125.8 %copy-start.54 = (f32[1152]{0:T(1024)}, f32[1152]{0:T(1024)S(1)}, u32[]{:S(2)}) copy-start(f32[1152]{0:T(1024)S(1)} %get-tuple-element.30) | copy-start | bytes 13828
  45.6 245.9 %copy-start.59 = (f32[1152]{0:T(1024)}, f32[1152]{0:T(1024)S(1)}, u32[]{:S(2)}) copy-start(f32[1152]{0:T(1024)S(1)} %get-tuple-element.31) | copy-start | bytes 13828
  45.6 247.8 %copy-start.48 = (f32[1152]{0:T(1024)}, f32[1152]{0:T(1024)S(1)}, u32[]{:S(2)}) copy-start(f32[1152]{0:T(1024)S(1)} %get-tuple-element.27) | copy-start | bytes 13828
  46.8 121.7 %reduce-scatter.9.cloned.1.call-start = ((), (), s32[]{:S(2)}) async-start(), calls=%async_computation.9 | async-start | bytes 5308416 | tf_op jit(solution)/shard_map/reduce_scatter | solution.py:94
  114.6 108.4 %all-gather.11.cloned.1.call-start = ((), (), s32[]{:S(2)}) async-start(), calls=%async_computation.10 | async-start | bytes 5308416 | tf_op jit(solution)/shard_map/all_gather | solution.py:90
  169.9 58.7 %copy-start.69 = (f32[256]{0:T(256)}, f32[256]{0:T(256)S(1)}, u32[]{:S(2)}) copy-start(f32[256]{0:T(256)S(1)} %broadcast_multiply_fusion.2) | copy-start | bytes 3076
  171.4 57.2 %copy-start.101 = (f32[256]{0:T(256)}, f32[256]{0:T(256)S(1)}, u32[]{:S(2)}) copy-start(f32[256]{0:T(256)S(1)} %multiply_reduce_fusion.9) | copy-start | bytes 3076
  171.4 57.2 %copy-start.80 = (f32[256]{0:T(256)}, f32[256]{0:T(256)S(1)}, u32[]{:S(2)}) copy-start(f32[256]{0:T(256)S(1)} %fusion.138) | copy-start | bytes 3076
  172.7 118.8 %reduce-scatter.11.cloned.1.call-start = ((), (), s32[]{:S(2)}) async-start(), calls=%async_computation.11 | async-start | bytes 5308416 | tf_op jit(solution)/shard_map/reduce_scatter | solution.py:94
  173.6 55.0 %copy-start.109 = (f32[576]{0:T(1024)}, f32[576]{0:T(1024)S(1)}, u32[]{:S(2)}) copy-start(f32[576]{0:T(1024)S(1)} %get-tuple-element.40) | copy-start | bytes 6916
  223.0 7.9 copy-start.116
  237.6 107.1 %all-gather.13.cloned.1.call-start = ((), (), s32[]{:S(2)}) async-start(), calls=%async_computation.12 | async-start | bytes 5308416 | tf_op jit(solution)/shard_map/all_gather | solution.py:90
  238.9 55.6 %copy-start.57 = (f32[1152]{0:T(1024)}, f32[1152]{0:T(1024)S(1)}, u32[]{:S(2)}) copy-start(f32[1152]{0:T(1024)S(1)} %get-tuple-element.36) | copy-start | bytes 13828
  293.0 51.7 %copy-start.37 = (bf16[1,1152,3,144]{1,3,2,0:T(8,128)(2,1)S(1)}, bf16[1,1152,3,144]{1,3,2,0:T(8,128)(2,1)}, u32[]{:S(2)}) copy-start(bf16[1,1152,3,144]{1,3,2,0:T(8,128)(2,1)} %get-tuple-element.78) | copy-start | bytes 2985988
  293.1 56.5 %copy-start.64 = (f32[256]{0:T(256)}, f32[256]{0:T(256)S(1)}, u32[]{:S(2)}) copy-start(f32[256]{0:T(256)S(1)} %broadcast_multiply_fusion.1) | copy-start | bytes 3076
  293.3 56.2 %copy-start.103 = (f32[256]{0:T(256)}, f32[256]{0:T(256)S(1)}, u32[]{:S(2)}) copy-start(f32[256]{0:T(256)S(1)} %multiply_reduce_fusion.8) | copy-start | bytes 3076
  293.4 56.2 %copy-start.76 = (f32[256]{0:T(256)}, f32[256]{0:T(256)S(1)}, u32[]{:S(2)}) copy-start(f32[256]{0:T(256)S(1)} %fusion.139) | copy-start | bytes 3076
  294.5 132.8 %reduce-scatter.13.cloned.1.call-start = ((), (), s32[]{:S(2)}) async-start(), calls=%async_computation.13 | async-start | bytes 5308416 | tf_op jit(solution)/shard_map/reduce_scatter | solution.py:94
  373.4 108.7 %all-gather.15.cloned.1.call-start = ((), (), s32[]{:S(2)}) async-start(), calls=%async_computation.14 | async-start | bytes 5308416 | tf_op jit(solution)/shard_map/all_gather | solution.py:90
  431.9 103.0 %all-gather.17.cloned.1.call-start = ((), (), s32[]{:S(2)}) async-start(), calls=%async_computation.16 | async-start | bytes 5308416 | tf_op jit(solution)/shard_map/all_gather | solution.py:100
  434.5 171.4 %reduce-scatter.17.cloned.1.call-start = ((), (), s32[]{:S(2)}) async-start(), calls=%async_computation.17 | async-start | bytes 5308416 | tf_op jit(solution)/shard_map/reduce_scatter | solution.py:104
  534.8 11.3 copy-start.117
  552.0 110.0 %reduce-scatter.15.cloned.1.call-start = ((), (), s32[]{:S(2)}) async-start(), calls=%async_computation.15 | async-start | bytes 5308416 | tf_op jit(solution)/shard_map/reduce_scatter | solution.py:94
  562.3 155.4 %all-gather.19.cloned.1.call-start = ((), (), s32[]{:S(2)}) async-start(), calls=%async_computation.18 | async-start | bytes 5308416 | tf_op jit(solution)/shard_map/all_gather | solution.py:100
  664.7 53.0 %copy-start.41 = (bf16[2,144,1152]{2,1,0:T(8,128)(2,1)S(1)}, bf16[2,144,1152]{2,1,0:T(8,128)(2,1)}, u32[]{:S(2)}) copy-start(bf16[2,144,1152]{2,1,0:T(8,128)(2,1)} %param.19) | copy-start | bytes 1990660
  664.7 53.0 %copy-start.82 = (f32[256]{0:T(256)}, f32[256]{0:T(256)S(1)}, u32[]{:S(2)}) copy-start(f32[256]{0:T(256)S(1)} %negate_multiply_fusion.3) | copy-start | bytes 3076
  667.5 135.6 %reduce-scatter.19.cloned.1.call-start = ((), (), s32[]{:S(2)}) async-start(), calls=%async_computation.19 | async-start | bytes 5308416 | tf_op jit(solution)/shard_map/reduce_scatter | solution.py:104
  749.2 58.3 %copy-start.3 = (f32[256,1152]{1,0:T(8,128)S(1)}, f32[256,1152]{1,0:T(8,128)}, u32[]{:S(2)}) copy-start(f32[256,1152]{1,0:T(8,128)} %copy-done.2) | copy-start | bytes 3538948
  749.2 111.1 %all-gather.21.cloned.1.call-start = ((), (), s32[]{:S(2)}) async-start(), calls=%async_computation.20 | async-start | bytes 5308416 | tf_op jit(solution)/shard_map/all_gather | solution.py:100
  810.1 121.3 %reduce-scatter.21.cloned.1.call-start = ((), (), s32[]{:S(2)}) async-start(), calls=%async_computation.21 | async-start | bytes 5308416 | tf_op jit(solution)/shard_map/reduce_scatter | solution.py:104
  860.3 11.3 copy-start.118
  877.4 54.0 %copy-start.55 = (f32[1152]{0:T(1024)S(1)}, f32[1152]{0:T(1024)}, u32[]{:S(2)}) copy-start(f32[1152]{0:T(1024)} %copy-done.54) | copy-start | bytes 13828
  877.4 54.0 %copy-start.70 = (f32[256]{0:T(256)S(1)}, f32[256]{0:T(256)}, u32[]{:S(2)}) copy-start(f32[256]{0:T(256)} %copy-done.69) | copy-start | bytes 3076
  877.4 54.0 %copy-start.81 = (f32[256]{0:T(256)S(1)}, f32[256]{0:T(256)}, u32[]{:S(2)}) copy-start(f32[256]{0:T(256)} %copy-done.80) | copy-start | bytes 3076
  877.4 56.3 %copy-start.102 = (f32[256]{0:T(256)S(1)}, f32[256]{0:T(256)}, u32[]{:S(2)}) copy-start(f32[256]{0:T(256)} %copy-done.101) | copy-start | bytes 3076
  877.5 56.9 %copy-start.7 = (f32[256,1152]{1,0:T(8,128)S(1)}, f32[256,1152]{1,0:T(8,128)}, u32[]{:S(2)}) copy-start(f32[256,1152]{1,0:T(8,128)} %get-tuple-element.58) | copy-start | bytes 3538948
  877.5 109.3 %all-gather.23.cloned.1.call-start = ((), (), s32[]{:S(2)}) async-start(), calls=%async_computation.22 | async-start | bytes 5308416 | tf_op jit(solution)/shard_map/all_gather | solution.py:100
  934.4 52.4 %copy-start.42 = (bf16[2,144,1152]{2,1,0:T(8,128)(2,1)S(1)}, bf16[2,144,1152]{2,1,0:T(8,128)(2,1)}, u32[]{:S(2)}) copy-start(bf16[2,144,1152]{2,1,0:T(8,128)(2,1)} %param.19) | copy-start | bytes 1990660
  936.5 54.5 %copy-start.63 = (f32[8,2,256]{2,1,0:T(2,128)S(1)}, f32[8,2,256]{2,1,0:T(2,128)}, u32[]{:S(2)}) copy-start(f32[8,2,256]{2,1,0:T(2,128)} %copy-done.62) | copy-start | bytes 49156
  936.5 130.9 %reduce-scatter.23.cloned.1.call-start = ((), (), s32[]{:S(2)}) async-start(), calls=%async_computation.23 | async-start | bytes 5308416 | tf_op jit(solution)/shard_map/reduce_scatter | solution.py:104
  1003.8 332.4 %all-reduce.5.cloned.1.call-start = ((), (), s32[]{:S(2)}) async-start(), calls=%async_computation.24 | async-start | bytes 23887872 | tf_op jit(solution)/shard_map/psum | solution.py:310
  1005.0 7.3 copy-start.111
  1012.4 9.2 copy-start.93
  1012.4 11.6 copy-start.4
  1012.4 11.6 copy-start.56
  1030.1 6.3 copy-start.87
  1030.1 6.5 copy-start.91
  1030.1 6.8 copy-start.90
  1030.1 7.1 copy-start.85
  1030.2 7.3 copy-start.89
  1030.2 7.8 copy-start.28
  1030.2 7.8 copy-start.58
  1038.2 6.5 copy-start.33
  1046.4 8.2 copy-start.32
  1070.9 30.2 %copy-start.108 = (f32[144]{0:T(256)S(1)}, f32[144]{0:T(256)}, u32[]{:S(2)}) copy-start(f32[144]{0:T(256)} %get-tuple-element.54) | copy-start | bytes 1732
  1338.4 6.0 copy-start.31
  (77 other events, 201.4 us)
Sparse Core Ops, SparseCore 0:
  46.9 49.9 all-gather.8
  114.7 53.7 reduce-scatter.8
  172.9 50.0 all-gather.10
  237.7 53.7 reduce-scatter.10
  294.6 50.0 all-gather.12
  373.5 53.7 reduce-scatter.12
  432.0 50.0 all-gather.14
  484.3 50.5 all-gather.16
  552.1 53.7 reduce-scatter.16
  608.7 53.3 reduce-scatter.14
  667.6 50.0 all-gather.18
  749.3 53.7 reduce-scatter.18
  810.2 50.0 all-gather.20
  877.6 53.7 reduce-scatter.20
  936.6 50.0 all-gather.22
  1003.9 53.7 reduce-scatter.22
  1103.7 232.4 all-reduce.4
where the time goes:
time: 1370 us; the launch traced here: 1360 us
  waiting for transfers between devices  959 us (70%)
  matrix products  176 us (13%)
  other arithmetic  82.1 us (6%)
  blocking collectives  76 us (6%)
  local copies, waits for them, and re-layouts  48.3 us (4%)
  between operations  16 us (1%)
    reduce_scatter x4, waiting for transfers between devices, reduce_rows(): lax.psum_scatter(partial_terms.astype(jnp.bfloat16), 'tensor', scatter_di...  212 us
    psum x1, waiting for transfers between devices, per_device(): lax.psum(ada_w_grad.astype(jnp.bfloat16), 'dp').astype(jnp.float32)  206 us
    all_gather x4, waiting for transfers between devices, spread_rows(): return lax.all_gather(row_block, 'tensor', axis=0, tiled=True)  195 us
    all_gather x4, waiting for transfers between devices, spread_grads(): return lax.all_gather(row_block, 'tensor', axis=0, tiled=True)  194 us
    reduce_scatter x4, waiting for transfers between devices, reduce_grads(): lax.psum_scatter(partial_terms.astype(jnp.bfloat16), 'tensor', scatter_di...  151 us
    psum x1, blocking collectives, per_device(): modulations = lax.psum(ada_terms, 'tensor') + ada_bias.astype(jnp.float32)  30.9 us
    unnamed x278, local copies, waits for them, and re-layouts  27.9 us
  transfers between devices with their start and end apart: 17, of which 16 were waited for; matrix products, arithmetic and copies ran while one was open for 7% of the time, Pallas kernels for 0%

commit v1 on v0

--- a/solution.py
+++ b/solution.py
@@ -8,6 +8,28 @@
 PATCHES = 256
 FRAMES = 8
 LAYERS = 2
+
+
+def in_order(parts, dim):
+    shape = list(parts.shape[1:])
+    shape[dim] *= parts.shape[0]
+    return jnp.moveaxis(parts, 0, dim).reshape(shape)
+
+
+def collect_2(array, axis, dim):
+    peers = lax.axis_size(axis)
+    pairs = [(i, (i + 1) % peers) for i in range(peers)]
+    back = [(b, a) for a, b in pairs]
+    lower, upper = ([], [])
+    for lap in range(peers - 1):
+        if lap % 2 == 0:
+            lower.append(lax.ppermute(lower[-1] if lower else array, axis, pairs))
+        else:
+            upper.append(lax.ppermute(upper[-1] if upper else array, axis, back))
+    blocks = jnp.stack([*lower[::-1], array, *upper])
+    shift = lax.axis_index(axis) - len(lower)
+    blocks = blocks[(jnp.arange(peers) - shift) % peers]
+    return in_order(blocks, dim)
 
 
 def normalize(stream):
@@ -87,7 +109,7 @@
 
 
 def spread_rows(row_block):
-    return lax.all_gather(row_block, "tensor", axis=0, tiled=True)
+    return collect_2(row_block, "tensor", 0)
 
 
 def reduce_rows(partial_terms):

time: 1370 us -> 1430 us (1.044)
  starting transfers between devices: 2.6 us -> 57.5 us
  local copies, waits for them, and re-layouts: 48.3 us -> 99.4 us
  waiting for transfers between devices: 959 us -> 911 us
    all_gather x4 -> x0, waiting for transfers between devices: 195 us -> none  [spread_rows(): return lax.all_gather(row_block, 'tensor', axis=0, tiled=True)]
    ppermute x0 -> x28, waiting for transfers between devices: none -> 194 us  [the longest x16 177 us: collect_2(): lower.append(lax.ppermute(lower[-1] if lower else array, axis, pairs))]
    ppermute x0 -> x28, starting transfers between devices: none -> 55.9 us  [the longest x12 55.7 us: collect_2(): upper.append(lax.ppermute(upper[-1] if upper else array, axis, back))]
    all_gather x4, waiting for transfers between devices: 194 us -> 150 us  [spread_grads(): return lax.all_gather(row_block, 'tensor', axis=0, tiled=True)]
    unnamed x278 -> x315, local copies, waits for them, and re-layouts: 27.9 us -> 53 us
    gather x0 -> x4, local copies, waits for them, and re-layouts: none -> 22.6 us  [collect_2(): blocks = blocks[(jnp.arange(peers) - shift) % peers]]
  transfers between devices with their start and end apart: 17 -> 41, of which waited for: 16 -> 34; matrix products, arithmetic and copies ran while one was open for 7% -> 9% of each run, Pallas kernels for 0% -> 0%
where the time goes in v1:
time: 1430 us; the launch traced here: 1420 us
  waiting for transfers between devices  911 us (64%)
  matrix products  176 us (12%)
  local copies, waits for them, and re-layouts  99.4 us (7%)
  other arithmetic  82 us (6%)
  blocking collectives  75.9 us (5%)
  starting transfers between devices  57.5 us (4%)
  between operations  15.7 us (1%)
    reduce_scatter x4, waiting for transfers between devices, reduce_rows(): lax.psum_scatter(partial_terms.astype(jnp.bfloat16), 'tensor', scatter_di...  207 us
    psum x1, waiting for transfers between devices, per_device(): lax.psum(ada_w_grad.astype(jnp.bfloat16), 'dp').astype(jnp.float32)  206 us
    ppermute x16, waiting for transfers between devices, collect_2(): lower.append(lax.ppermute(lower[-1] if lower else array, axis, pairs))  177 us
    reduce_scatter x4, waiting for transfers between devices, reduce_grads(): lax.psum_scatter(partial_terms.astype(jnp.bfloat16), 'tensor', scatter_di...  154 us
    all_gather x4, waiting for transfers between devices, spread_grads(): return lax.all_gather(row_block, 'tensor', axis=0, tiled=True)  150 us
    ppermute x12, starting transfers between devices, collect_2(): upper.append(lax.ppermute(upper[-1] if upper else array, axis, back))  55.7 us
    unnamed x315, local copies, waits for them, and re-layouts  53 us
    psum x1, blocking collectives, per_device(): modulations = lax.psum(ada_terms, 'tensor') + ada_bias.astype(jnp.float32)  30.7 us
  transfers between devices with their start and end apart: 41, of which 34 were waited for; matrix products, arithmetic and copies ran while one was open for 9% of the time, Pallas kernels for 0%

profile of v1, /device:TPU:0, one launch (start us, length us, event | category | flops | bytes accessed | tf_op | source)
XLA Modules:
  0.0 1417.2 jit_solution(10159458523506002125)
XLA Ops:
  14.1 30.7 %psum.98 = f32[2,6912]{1,0:T(2,128)S(1)} all-reduce(f32[2,6912]{1,0:T(2,128)S(1)} %bitcast.448), channel_id=1, replica_groups=mesh['dp'=4,'tensor'=8] {'tensor'}, use_global_device_ids=true, to_apply=%region_0.1 | all-reduce | flops 13824 | bytes 110592 | tf_op jit(solution)/shard_map/psum | solution.py:285
  46.7 11.5 collective-permute-done
  61.7 10.8 collective-permute-done.1
  78.3 8.5 collective-permute-done.2
  95.4 6.5 collective-permute-done.3
  112.3 5.7 gather_fusion
  117.9 4.8 fusion.190
  131.5 3.8 convolution_convert_fusion.7
  136.6 52.0 %reduce-scatter.9.cloned.1.call-done = bf16[256,1152]{1,0:T(8,128)(2,1)} async-done(((bf16[2048,1152]{1,0:T(8,128)(2,1)}), bf16[256,1152]{1,0:T(8,128)(2,1)}) %reduce-scatter.9.cloned.1.call-update) | async-done | bytes 589840 | tf_op jit(solution)/shard_map/reduce_scatter | solution.py:116
  192.1 11.1 collective-permute-done.7
  206.8 11.5 collective-permute-done.8
  218.8 3.7 collective-permute-start.12
  222.6 9.6 collective-permute-done.9
  236.1 4.1 collective-permute-start.13
  240.2 6.5 collective-permute-done.10
  253.7 5.6 gather_fusion.1
  259.3 5.6 fusion.61
  267.1 6.7 convolution_convert_fusion.6
  275.1 51.9 %reduce-scatter.11.cloned.1.call-done = bf16[256,1152]{1,0:T(8,128)(2,1)} async-done(((bf16[2048,1152]{1,0:T(8,128)(2,1)}), bf16[256,1152]{1,0:T(8,128)(2,1)}) %reduce-scatter.11.cloned.1.call-update) | async-done | bytes 589840 | tf_op jit(solution)/shard_map/reduce_scatter | solution.py:116
  329.2 11.1 collective-permute-done.14
  343.9 11.5 collective-permute-done.15
  359.7 9.6 collective-permute-done.16
  369.2 4.0 collective-permute-done.19
  373.2 3.8 collective-permute-start.20
  377.0 5.9 collective-permute-done.17
  390.1 5.7 gather_fusion.2
  395.8 4.8 fusion.191
  407.7 5.4 fusion.178
  419.8 4.8 convolution_convert_fusion.5
  427.2 50.6 %reduce-scatter.13.cloned.1.call-done = bf16[256,1152]{1,0:T(8,128)(2,1)} async-done(((bf16[2048,1152]{1,0:T(8,128)(2,1)}), bf16[256,1152]{1,0:T(8,128)(2,1)}) %reduce-scatter.13.cloned.1.call-update) | async-done | bytes 589840 | tf_op jit(solution)/shard_map/reduce_scatter | solution.py:116
  481.1 14.3 %collective-permute-done.21 = bf16[256,1152]{1,0:T(8,128)(2,1)S(1)} collective-permute-done((bf16[256,1152]{1,0:T(8,128)(2,1)S(1)}, bf16[256,1152]{1,0:T(8,128)(2,1)S(1)}, u32[]{:S(2)}, u32[]{:S(2)}) %collective-permute-start.21) | collective-permute-done | bytes 589856 | tf_op jit(solution)/shard_map/ppermute | solution.py:26
  498.9 25.3 %collective-permute-done.22 = bf16[256,1152]{1,0:T(8,128)(2,1)S(1)} collective-permute-done((bf16[256,1152]{1,0:T(8,128)(2,1)S(1)}, bf16[256,1152]{1,0:T(8,128)(2,1)S(1)}, u32[]{:S(2)}, u32[]{:S(2)}) %collective-permute-start.22) | collective-permute-done | bytes 589856 | tf_op jit(solution)/shard_map/ppermute | solution.py:26
  524.2 3.7 collective-permute-start.26
  528.0 22.9 %collective-permute-done.23 = bf16[256,1152]{1,0:T(8,128)(2,1)S(1)} collective-permute-done((bf16[256,1152]{1,0:T(8,128)(2,1)S(1)}, bf16[256,1152]{1,0:T(8,128)(2,1)S(1)}, u32[]{:S(2)}, u32[]{:S(2)}) %collective-permute-start.23) | collective-permute-done | bytes 589856 | tf_op jit(solution)/shard_map/ppermute | solution.py:26
  553.0 15.1 %collective-permute-start.27 = (bf16[256,1152]{1,0:T(8,128)(2,1)S(1)}, bf16[256,1152]{1,0:T(8,128)(2,1)S(1)}, u32[]{:S(2)}, u32[]{:S(2)}) collective-permute-start(bf16[256,1152]{1,0:T(8,128)(2,1)S(1)} %collective-permute-done.26), channel_id=1, source_target_pairs={{1,0},{2,1},{3,2},{4,3},{5,4},{6,5},{7,6},{0,7},{9,8},{10,9},{11,1... | collective-permute-start | bytes 1769480 | tf_op jit(solution)/shard_map/ppermute | solution.py:28
  576.4 5.6 gather_fusion.3
  582.0 8.2 fusion.53
  590.2 9.9 fusion.187
  601.5 5.8 convolution_convert_fusion.3
  607.4 10.0 convolution_convert_fusion.4
  617.5 46.3 %reduce-scatter.17.cloned.1.call-done = bf16[256,1152]{1,0:T(8,128)(2,1)} async-done(((bf16[2048,1152]{1,0:T(8,128)(2,1)}), bf16[256,1152]{1,0:T(8,128)(2,1)}) %reduce-scatter.17.cloned.1.call-update) | async-done | bytes 589840 | tf_op jit(solution)/shard_map/reduce_scatter | solution.py:126
  667.2 52.1 %reduce-scatter.15.cloned.1.call-done = bf16[256,1152]{1,0:T(8,128)(2,1)} async-done(((bf16[2048,1152]{1,0:T(8,128)(2,1)}), bf16[256,1152]{1,0:T(8,128)(2,1)}) %reduce-scatter.15.cloned.1.call-update) | async-done | bytes 589840 | tf_op jit(solution)/shard_map/reduce_scatter | solution.py:116
  725.0 50.0 %all-gather.7.cloned.1.call-done = bf16[2048,1152]{1,0:T(8,128)(2,1)} async-done(((bf16[256,1152]{1,0:T(8,128)(2,1)}), bf16[2048,1152]{1,0:T(8,128)(2,1)}) %all-gather.7.cloned.1.call-update) | async-done | bytes 4718608 | tf_op jit(solution)/shard_map/all_gather | solution.py:122
  775.0 4.0 convolution_convert_fusion.17
  780.9 4.3 fusion.183
  801.9 4.6 convolution_convert_fusion.1
  806.5 53.9 %reduce-scatter.19.cloned.1.call-done = bf16[256,1152]{1,0:T(8,128)(2,1)} async-done(((bf16[2048,1152]{1,0:T(8,128)(2,1)}), bf16[256,1152]{1,0:T(8,128)(2,1)}) %reduce-scatter.19.cloned.1.call-update) | async-done | bytes 589840 | tf_op jit(solution)/shard_map/reduce_scatter | solution.py:126
  867.8 49.8 %all-gather.9.cloned.1.call-done = bf16[2048,1152]{1,0:T(8,128)(2,1)} async-done(((bf16[256,1152]{1,0:T(8,128)(2,1)}), bf16[2048,1152]{1,0:T(8,128)(2,1)}) %all-gather.9.cloned.1.call-update) | async-done | bytes 4718608 | tf_op jit(solution)/shard_map/all_gather | solution.py:122
  917.6 9.9 fusion.188
  928.8 5.8 convolution_convert_fusion.2
  934.7 53.8 %reduce-scatter.21.cloned.1.call-done = bf16[256,1152]{1,0:T(8,128)(2,1)} async-done(((bf16[2048,1152]{1,0:T(8,128)(2,1)}), bf16[256,1152]{1,0:T(8,128)(2,1)}) %reduce-scatter.21.cloned.1.call-update) | async-done | bytes 589840 | tf_op jit(solution)/shard_map/reduce_scatter | solution.py:126
  993.9 50.0 %all-gather.11.cloned.1.call-done = bf16[2048,1152]{1,0:T(8,128)(2,1)} async-done(((bf16[256,1152]{1,0:T(8,128)(2,1)}), bf16[2048,1152]{1,0:T(8,128)(2,1)}) %all-gather.11.cloned.1.call-update) | async-done | bytes 4718608 | tf_op jit(solution)/shard_map/all_gather | solution.py:122
  1043.9 4.1 convolution_convert_fusion.16
  1056.3 4.6 convolution_convert_fusion
  1062.2 7.3 fusion.22
  1069.5 9.2 fusion.20
  1087.3 5.9 fusion.24
  1095.4 6.4 fusion.21
  1103.6 8.2 fusion.19
  1118.3 4.9 fusion.23
  1131.6 26.9 %all-reduce = (bf16[2,6912]{1,0:T(2,128)(2,1)S(1)}, bf16[2,1152]{1,0:T(2,128)(2,1)S(1)}, bf16[2,1152]{1,0:T(2,128)(2,1)S(1)}) all-reduce(bf16[2,6912]{1,0:T(2,128)(2,1)S(1)} %pad_maximum_fusion.4, bf16[2,1152]{1,0:T(2,128)(2,1)S(1)} %get-tuple-element.108, ...), channel_id=1, replica_groups=mesh['dp'=4,'tensor'=8] {'tensor'}, use_global_device_ids=true, to_apply=%region_43.44 | all-reduce | flops 18432 | bytes 73728 | tf_op jit(solution)/shard_map/psum | solution.py:320
  1166.0 18.3 %all-reduce.1 = (bf16[2,6912]{1,0:T(2,128)(2,1)S(1)}, bf16[2,2,144]{2,1,0:T(2,128)(2,1)S(1)}, bf16[2,1152]{1,0:T(2,128)(2,1)S(1)}, bf16[2,576]{1,0:T(2,128)(2,1)S(1)}, bf16[2,1152]{1,0:T(2,128)(2,1)S(1)}) all-reduce(bf16[2,6912]{1,0:T(2,128)(2,1)S(1)} %get-tuple-element.41, ...), channel_id=1, replica_groups=mesh['dp'=4,'tensor'=8] {'dp'}, use_global_device_ids=true, to_apply=%region_45.46 | all-reduce | flops 20160 | bytes 80640 | tf_op jit(solution)/shard_map/psum | solution.py:333
  1187.3 206.3 %all-reduce.5.cloned.1.call-done = (bf16[2,144,6912]{2,1,0:T(8,128)(2,1)}, bf16[2,1152,3,144]{1,3,2,0:T(8,128)(2,1)}, bf16[2,144,1152]{2,1,0:T(8,128)(2,1)}, bf1...) async-done(((bf16[2,144,6912]{2,1,0:T(8,128)(2,1)}, bf16[2,1152,3,144]{1,3,2,0:T(8,128)(2,1)}, bf16[2,144,1152]{2,1,0:T(8,128)(2,1)}, bf16[2,1152,576]{1,2,0:T(8,128)(2,1)}, ...) | async-done | bytes 11943952 | tf_op jit(solution)/shard_map/psum | solution.py:332
  1395.9 6.0 convert_element_type.432
  (517 shorter events, 220.1 us)
Async XLA Ops:
  7.2 181.5 %reduce-scatter.9.cloned.1.call-start = ((), (), s32[]{:S(2)}) async-start(), calls=%async_computation.8 | async-start | bytes 5308416 | tf_op jit(solution)/shard_map/reduce_scatter | solution.py:116
  9.1 98.4 %copy-start.71 = (f32[256]{0:T(256)}, f32[256]{0:T(256)S(1)}, u32[]{:S(2)}) copy-start(f32[256]{0:T(256)S(1)} %broadcast_multiply_fusion.3) | copy-start | bytes 3076
  10.5 97.0 %copy-start.77 = (f32[256]{0:T(256)}, f32[256]{0:T(256)S(1)}, u32[]{:S(2)}) copy-start(f32[256]{0:T(256)S(1)} %fusion.144) | copy-start | bytes 3076
  11.1 61.4 %copy-start.113 = (bf16[2,2,144]{2,1,0:T(2,128)(2,1)S(1)}, bf16[2,2,144]{2,1,0:T(2,128)(2,1)}, u32[]{:S(2)}) copy-start(bf16[2,2,144]{2,1,0:T(2,128)(2,1)} %param.18) | copy-start | bytes 3460
  11.1 75.6 %copy-start.31 = (bf16[2,1152,3,144]{1,3,2,0:T(8,128)(2,1)S(1)}, bf16[2,1152,3,144]{1,3,2,0:T(8,128)(2,1)}, u32[]{:S(2)}) copy-start(bf16[2,1152,3,144]{1,3,2,0:T(8,128)(2,1)} %param.17) | copy-start | bytes 5971972
  45.6 61.9 %copy-start.47 = (f32[1152]{0:T(1024)}, f32[1152]{0:T(1024)S(1)}, u32[]{:S(2)}) copy-start(f32[1152]{0:T(1024)S(1)} %get-tuple-element.33) | copy-start | bytes 13828
  45.6 146.0 %copy-start.57 = (f32[1152]{0:T(1024)}, f32[1152]{0:T(1024)S(1)}, u32[]{:S(2)}) copy-start(f32[1152]{0:T(1024)S(1)} %get-tuple-element.30) | copy-start | bytes 13828
  45.6 281.4 %copy-start.60 = (f32[1152]{0:T(1024)}, f32[1152]{0:T(1024)S(1)}, u32[]{:S(2)}) copy-start(f32[1152]{0:T(1024)S(1)} %get-tuple-element.31) | copy-start | bytes 13828
  45.6 340.8 %copy-start.49 = (f32[1152]{0:T(1024)}, f32[1152]{0:T(1024)S(1)}, u32[]{:S(2)}) copy-start(f32[1152]{0:T(1024)S(1)} %get-tuple-element.27) | copy-start | bytes 13828
  46.7 11.5 collective-permute-start
  58.2 14.3 %collective-permute-start.1 = (bf16[256,1152]{1,0:T(8,128)(2,1)S(1)}, bf16[256,1152]{1,0:T(8,128)(2,1)}, u32[]{:S(2)}, u32[]{:S(2)}) collective-permute-start(bf16[256,1152]{1,0:T(8,128)(2,1)S(1)} %collective-permute-done), channel_id=1, source_target_pairs={{0,1},{1,2},{2,3},{3,4},{4,5},{5,6},{6,7},{7,0},{8,9},{9,10},{10,1... | collective-permute-start | bytes 1769480 | tf_op jit(solution)/shard_map/ppermute | solution.py:26
  58.2 16.4 %collective-permute-start.4 = (bf16[256,1152]{1,0:T(8,128)(2,1)}, bf16[256,1152]{1,0:T(8,128)(2,1)}, u32[]{:S(2)}, u32[]{:S(2)}) collective-permute-start(bf16[256,1152]{1,0:T(8,128)(2,1)} %fusion.70), channel_id=1, source_target_pairs={{1,0},{2,1},{3,2},{4,3},{5,4},{6,5},{7,6},{0,7},{9,8},{10,9},{11,1... | collective-permute-start | bytes 1769480 | tf_op jit(solution)/shard_map/ppermute | solution.py:28
  72.5 14.2 %collective-permute-start.2 = (bf16[256,1152]{1,0:T(8,128)(2,1)}, bf16[256,1152]{1,0:T(8,128)(2,1)}, u32[]{:S(2)}, u32[]{:S(2)}) collective-permute-start(bf16[256,1152]{1,0:T(8,128)(2,1)} %collective-permute-done.1), channel_id=1, source_target_pairs={{0,1},{1,2},{2,3},{3,4},{4,5},{5,6},{6,7},{7,0},{8,9},{9,10},{10,1... | collective-permute-start | bytes 1769480 | tf_op jit(solution)/shard_map/ppermute | solution.py:26
  74.6 17.2 %collective-permute-start.5 = (bf16[256,1152]{1,0:T(8,128)(2,1)}, bf16[256,1152]{1,0:T(8,128)(2,1)S(1)}, u32[]{:S(2)}, u32[]{:S(2)}) collective-permute-start(bf16[256,1152]{1,0:T(8,128)(2,1)} %collective-permute-done.4), channel_id=1, source_target_pairs={{1,0},{2,1},{3,2},{4,3},{5,4},{6,5},{7,6},{0,7},{9,8},{10,9},{11,1... | collective-permute-start | bytes 1769480 | tf_op jit(solution)/shard_map/ppermute | solution.py:28
  86.7 15.2 %collective-permute-start.3 = (bf16[256,1152]{1,0:T(8,128)(2,1)}, bf16[256,1152]{1,0:T(8,128)(2,1)S(1)}, u32[]{:S(2)}, u32[]{:S(2)}) collective-permute-start(bf16[256,1152]{1,0:T(8,128)(2,1)} %collective-permute-done.2), channel_id=1, source_target_pairs={{0,1},{1,2},{2,3},{3,4},{4,5},{5,6},{6,7},{7,0},{8,9},{9,10},{10,1... | collective-permute-start | bytes 1769480 | tf_op jit(solution)/shard_map/ppermute | solution.py:26
  86.8 303.3 %copy-start.110 = (s32[1024]{0:T(1024)}, s32[1024]{0:T(1024)S(1)}, u32[]{:S(2)}) copy-start(s32[1024]{0:T(1024)S(1)} %pad_clamp_fusion) | copy-start | bytes 12292
  91.7 19.6 %collective-permute-start.6 = (bf16[256,1152]{1,0:T(8,128)(2,1)S(1)}, bf16[256,1152]{1,0:T(8,128)(2,1)S(1)}, u32[]{:S(2)}, u32[]{:S(2)}) collective-permute-start(bf16[256,1152]{1,0:T(8,128)(2,1)S(1)} %collective-permute-done.5), channel_id=1, source_target_pairs={{1,0},{2,1},{3,2},{4,3},{5,4},{6,5},{7,6},{0,7},{9,8},{10,9},{11,1... | collective-permute-start | bytes 1769480 | tf_op jit(solution)/shard_map/ppermute | solution.py:28
  135.3 191.7 %reduce-scatter.11.cloned.1.call-start = ((), (), s32[]{:S(2)}) async-start(), calls=%async_computation.9 | async-start | bytes 5308416 | tf_op jit(solution)/shard_map/reduce_scatter | solution.py:116
  190.1 57.6 %copy-start.79 = (f32[256]{0:T(256)}, f32[256]{0:T(256)S(1)}, u32[]{:S(2)}) copy-start(f32[256]{0:T(256)S(1)} %broadcast_multiply_fusion.2) | copy-start | bytes 3076
  191.6 57.8 %copy-start.106 = (f32[256]{0:T(256)}, f32[256]{0:T(256)S(1)}, u32[]{:S(2)}) copy-start(f32[256]{0:T(256)S(1)} %multiply_reduce_fusion.9) | copy-start | bytes 3076
  191.6 57.8 %copy-start.86 = (f32[256]{0:T(256)}, f32[256]{0:T(256)S(1)}, u32[]{:S(2)}) copy-start(f32[256]{0:T(256)S(1)} %fusion.145) | copy-start | bytes 3076
  192.0 11.2 collective-permute-start.7
  203.2 15.1 %collective-permute-start.8 = (bf16[256,1152]{1,0:T(8,128)(2,1)S(1)}, bf16[256,1152]{1,0:T(8,128)(2,1)S(1)}, u32[]{:S(2)}, u32[]{:S(2)}) collective-permute-start(bf16[256,1152]{1,0:T(8,128)(2,1)S(1)} %collective-permute-done.7), channel_id=1, source_target_pairs={{0,1},{1,2},{2,3},{3,4},{4,5},{5,6},{6,7},{7,0},{8,9},{9,10},{10,1... | collective-permute-start | bytes 1769480 | tf_op jit(solution)/shard_map/ppermute | solution.py:26
  203.2 15.6 %collective-permute-start.11 = (bf16[256,1152]{1,0:T(8,128)(2,1)S(1)}, bf16[256,1152]{1,0:T(8,128)(2,1)S(1)}, u32[]{:S(2)}, u32[]{:S(2)}) collective-permute-start(bf16[256,1152]{1,0:T(8,128)(2,1)S(1)} %add_convert_fusion.4), channel_id=1, source_target_pairs={{1,0},{2,1},{3,2},{4,3},{5,4},{6,5},{7,6},{0,7},{9,8},{10,9},{11,1... | collective-permute-start | bytes 1769480 | tf_op jit(solution)/shard_map/ppermute | solution.py:28
  218.3 13.8 collective-permute-start.9
  218.8 17.3 %collective-permute-start.12 = (bf16[256,1152]{1,0:T(8,128)(2,1)S(1)}, bf16[256,1152]{1,0:T(8,128)(2,1)S(1)}, u32[]{:S(2)}, u32[]{:S(2)}) collective-permute-start(bf16[256,1152]{1,0:T(8,128)(2,1)S(1)} %collective-permute-done.11), channel_id=1, source_target_pairs={{1,0},{2,1},{3,2},{4,3},{5,4},{6,5},{7,6},{0,7},{9,8},{10,9},{11,1... | collective-permute-start | bytes 1769480 | tf_op jit(solution)/shard_map/ppermute | solution.py:28
  232.1 14.6 %collective-permute-start.10 = (bf16[256,1152]{1,0:T(8,128)(2,1)S(1)}, bf16[256,1152]{1,0:T(8,128)(2,1)S(1)}, u32[]{:S(2)}, u32[]{:S(2)}) collective-permute-start(bf16[256,1152]{1,0:T(8,128)(2,1)S(1)} %collective-permute-done.9), channel_id=1, source_target_pairs={{0,1},{1,2},{2,3},{3,4},{4,5},{5,6},{6,7},{7,0},{8,9},{9,10},{10,1... | collective-permute-start | bytes 1769480 | tf_op jit(solution)/shard_map/ppermute | solution.py:26
  236.1 16.7 %collective-permute-start.13 = (bf16[256,1152]{1,0:T(8,128)(2,1)S(1)}, bf16[256,1152]{1,0:T(8,128)(2,1)S(1)}, u32[]{:S(2)}, u32[]{:S(2)}) collective-permute-start(bf16[256,1152]{1,0:T(8,128)(2,1)S(1)} %collective-permute-done.12), channel_id=1, source_target_pairs={{1,0},{2,1},{3,2},{4,3},{5,4},{6,5},{7,6},{0,7},{9,8},{10,9},{11,1... | collective-permute-start | bytes 1769480 | tf_op jit(solution)/shard_map/ppermute | solution.py:28
  273.8 204.0 %reduce-scatter.13.cloned.1.call-start = ((), (), s32[]{:S(2)}) async-start(), calls=%async_computation.10 | async-start | bytes 5308416 | tf_op jit(solution)/shard_map/reduce_scatter | solution.py:116
  328.5 57.9 %copy-start.69 = (f32[256]{0:T(256)}, f32[256]{0:T(256)S(1)}, u32[]{:S(2)}) copy-start(f32[256]{0:T(256)S(1)} %broadcast_multiply_fusion.1) | copy-start | bytes 3076
  328.8 56.8 %copy-start.108 = (f32[256]{0:T(256)}, f32[256]{0:T(256)S(1)}, u32[]{:S(2)}) copy-start(f32[256]{0:T(256)S(1)} %multiply_reduce_fusion.8) | copy-start | bytes 3076
  328.8 57.6 %copy-start.75 = (f32[256]{0:T(256)}, f32[256]{0:T(256)S(1)}, u32[]{:S(2)}) copy-start(f32[256]{0:T(256)S(1)} %fusion.146) | copy-start | bytes 3076
  329.1 11.2 collective-permute-start.14
  340.3 15.1 %collective-permute-start.15 = (bf16[256,1152]{1,0:T(8,128)(2,1)S(1)}, bf16[256,1152]{1,0:T(8,128)(2,1)S(1)}, u32[]{:S(2)}, u32[]{:S(2)}) collective-permute-start(bf16[256,1152]{1,0:T(8,128)(2,1)S(1)} %collective-permute-done.14), channel_id=1, source_target_pairs={{0,1},{1,2},{2,3},{3,4},{4,5},{5,6},{6,7},{7,0},{8,9},{9,10},{10,1... | collective-permute-start | bytes 1769480 | tf_op jit(solution)/shard_map/ppermute | solution.py:26
  340.3 15.6 %collective-permute-start.18 = (bf16[256,1152]{1,0:T(8,128)(2,1)S(1)}, bf16[256,1152]{1,0:T(8,128)(2,1)S(1)}, u32[]{:S(2)}, u32[]{:S(2)}) collective-permute-start(bf16[256,1152]{1,0:T(8,128)(2,1)S(1)} %add_convert_fusion.3), channel_id=1, source_target_pairs={{1,0},{2,1},{3,2},{4,3},{5,4},{6,5},{7,6},{0,7},{9,8},{10,9},{11,1... | collective-permute-start | bytes 1769480 | tf_op jit(solution)/shard_map/ppermute | solution.py:28
  355.4 13.8 collective-permute-start.16
  356.0 17.2 %collective-permute-start.19 = (bf16[256,1152]{1,0:T(8,128)(2,1)S(1)}, bf16[256,1152]{1,0:T(8,128)(2,1)S(1)}, u32[]{:S(2)}, u32[]{:S(2)}) collective-permute-start(bf16[256,1152]{1,0:T(8,128)(2,1)S(1)} %collective-permute-done.18), channel_id=1, source_target_pairs={{1,0},{2,1},{3,2},{4,3},{5,4},{6,5},{7,6},{0,7},{9,8},{10,9},{11,1... | collective-permute-start | bytes 1769480 | tf_op jit(solution)/shard_map/ppermute | solution.py:28
  369.2 13.7 collective-permute-start.17
  373.2 16.0 %collective-permute-start.20 = (bf16[256,1152]{1,0:T(8,128)(2,1)S(1)}, bf16[256,1152]{1,0:T(8,128)(2,1)S(1)}, u32[]{:S(2)}, u32[]{:S(2)}) collective-permute-start(bf16[256,1152]{1,0:T(8,128)(2,1)S(1)} %collective-permute-done.19), channel_id=1, source_target_pairs={{1,0},{2,1},{3,2},{4,3},{5,4},{6,5},{7,6},{0,7},{9,8},{10,9},{11,1... | collective-permute-start | bytes 1769480 | tf_op jit(solution)/shard_map/ppermute | solution.py:28
  424.5 165.7 %all-gather.5.cloned.1.call-start = ((), (), s32[]{:S(2)}) async-start(), calls=%async_computation.12 | async-start | bytes 5308416 | tf_op jit(solution)/shard_map/all_gather | solution.py:122
  427.1 236.6 %reduce-scatter.17.cloned.1.call-start = ((), (), s32[]{:S(2)}) async-start(), calls=%async_computation.13 | async-start | bytes 5308416 | tf_op jit(solution)/shard_map/reduce_scatter | solution.py:126
  479.1 92.4 %copy-start.73 = (f32[256]{0:T(256)}, f32[256]{0:T(256)S(1)}, u32[]{:S(2)}) copy-start(f32[256]{0:T(256)S(1)} %broadcast_multiply_fusion) | copy-start | bytes 3076
  479.4 92.2 %copy-start.81 = (f32[256]{0:T(256)}, f32[256]{0:T(256)S(1)}, u32[]{:S(2)}) copy-start(f32[256]{0:T(256)S(1)} %fusion.147) | copy-start | bytes 3076
  481.0 90.6 %copy-start.52 = (f32[1152]{0:T(1024)S(1)}, f32[1152]{0:T(1024)}, u32[]{:S(2)}) copy-start(f32[1152]{0:T(1024)} %get-tuple-element.25) | copy-start | bytes 13828
  481.0 90.6 %copy-start.66 = (f32[1152]{0:T(1024)S(1)}, f32[1152]{0:T(1024)}, u32[]{:S(2)}) copy-start(f32[1152]{0:T(1024)} %get-tuple-element.24) | copy-start | bytes 13828
  481.0 14.4 %collective-permute-start.21 = (bf16[256,1152]{1,0:T(8,128)(2,1)S(1)}, bf16[256,1152]{1,0:T(8,128)(2,1)S(1)}, u32[]{:S(2)}, u32[]{:S(2)}) collective-permute-start(bf16[256,1152]{1,0:T(8,128)(2,1)S(1)} %add_convert_fusion.2), channel_id=1, source_target_pairs={{0,1},{1,2},{2,3},{3,4},{4,5},{5,6},{6,7},{7,0},{8,9},{9,10},{10,1... | collective-permute-start | bytes 1769480 | tf_op jit(solution)/shard_map/ppermute | solution.py:26
  495.4 28.8 %collective-permute-start.22 = (bf16[256,1152]{1,0:T(8,128)(2,1)S(1)}, bf16[256,1152]{1,0:T(8,128)(2,1)S(1)}, u32[]{:S(2)}, u32[]{:S(2)}) collective-permute-start(bf16[256,1152]{1,0:T(8,128)(2,1)S(1)} %collective-permute-done.21), channel_id=1, source_target_pairs={{0,1},{1,2},{2,3},{3,4},{4,5},{5,6},{6,7},{7,0},{8,9},{9,10},{10,1... | collective-permute-start | bytes 1769480 | tf_op jit(solution)/shard_map/ppermute | solution.py:26
  495.4 28.9 %collective-permute-start.25 = (bf16[256,1152]{1,0:T(8,128)(2,1)S(1)}, bf16[256,1152]{1,0:T(8,128)(2,1)S(1)}, u32[]{:S(2)}, u32[]{:S(2)}) collective-permute-start(bf16[256,1152]{1,0:T(8,128)(2,1)S(1)} %add_convert_fusion.2), channel_id=1, source_target_pairs={{1,0},{2,1},{3,2},{4,3},{5,4},{6,5},{7,6},{0,7},{9,8},{10,9},{11,1... | collective-permute-start | bytes 1769480 | tf_op jit(solution)/shard_map/ppermute | solution.py:28
  524.2 26.7 %collective-permute-start.23 = (bf16[256,1152]{1,0:T(8,128)(2,1)S(1)}, bf16[256,1152]{1,0:T(8,128)(2,1)S(1)}, u32[]{:S(2)}, u32[]{:S(2)}) collective-permute-start(bf16[256,1152]{1,0:T(8,128)(2,1)S(1)} %collective-permute-done.22), channel_id=1, source_target_pairs={{0,1},{1,2},{2,3},{3,4},{4,5},{5,6},{6,7},{7,0},{8,9},{9,10},{10,1... | collective-permute-start | bytes 1769480 | tf_op jit(solution)/shard_map/ppermute | solution.py:26
  524.2 28.8 %collective-permute-start.26 = (bf16[256,1152]{1,0:T(8,128)(2,1)S(1)}, bf16[256,1152]{1,0:T(8,128)(2,1)S(1)}, u32[]{:S(2)}, u32[]{:S(2)}) collective-permute-start(bf16[256,1152]{1,0:T(8,128)(2,1)S(1)} %collective-permute-done.25), channel_id=1, source_target_pairs={{1,0},{2,1},{3,2},{4,3},{5,4},{6,5},{7,6},{0,7},{9,8},{10,9},{11,1... | collective-permute-start | bytes 1769480 | tf_op jit(solution)/shard_map/ppermute | solution.py:28
  550.9 17.2 %collective-permute-start.24 = (bf16[256,1152]{1,0:T(8,128)(2,1)S(1)}, bf16[256,1152]{1,0:T(8,128)(2,1)S(1)}, u32[]{:S(2)}, u32[]{:S(2)}) collective-permute-start(bf16[256,1152]{1,0:T(8,128)(2,1)S(1)} %collective-permute-done.23), channel_id=1, source_target_pairs={{0,1},{1,2},{2,3},{3,4},{4,5},{5,6},{6,7},{7,0},{8,9},{9,10},{10,1... | collective-permute-start | bytes 1769480 | tf_op jit(solution)/shard_map/ppermute | solution.py:26
  553.0 22.5 %collective-permute-start.27 = (bf16[256,1152]{1,0:T(8,128)(2,1)S(1)}, bf16[256,1152]{1,0:T(8,128)(2,1)S(1)}, u32[]{:S(2)}, u32[]{:S(2)}) collective-permute-start(bf16[256,1152]{1,0:T(8,128)(2,1)S(1)} %collective-permute-done.26), channel_id=1, source_target_pairs={{1,0},{2,1},{3,2},{4,3},{5,4},{6,5},{7,6},{0,7},{9,8},{10,9},{11,1... | collective-permute-start | bytes 1769480 | tf_op jit(solution)/shard_map/ppermute | solution.py:28
  607.3 111.9 %reduce-scatter.15.cloned.1.call-start = ((), (), s32[]{:S(2)}) async-start(), calls=%async_computation.11 | async-start | bytes 5308416 | tf_op jit(solution)/shard_map/reduce_scatter | solution.py:116
  617.5 157.5 %all-gather.7.cloned.1.call-start = ((), (), s32[]{:S(2)}) async-start(), calls=%async_computation.14 | async-start | bytes 5308416 | tf_op jit(solution)/shard_map/all_gather | solution.py:122
  724.7 135.7 %reduce-scatter.19.cloned.1.call-start = ((), (), s32[]{:S(2)}) async-start(), calls=%async_computation.15 | async-start | bytes 5308416 | tf_op jit(solution)/shard_map/reduce_scatter | solution.py:126
  806.5 58.3 %copy-start.3 = (f32[256,1152]{1,0:T(8,128)S(1)}, f32[256,1152]{1,0:T(8,128)}, u32[]{:S(2)}) copy-start(f32[256,1152]{1,0:T(8,128)} %copy-done.2) | copy-start | bytes 3538948
  806.5 111.1 %all-gather.9.cloned.1.call-start = ((), (), s32[]{:S(2)}) async-start(), calls=%async_computation.16 | async-start | bytes 5308416 | tf_op jit(solution)/shard_map/all_gather | solution.py:122
  867.4 121.2 %reduce-scatter.21.cloned.1.call-start = ((), (), s32[]{:S(2)}) async-start(), calls=%async_computation.17 | async-start | bytes 5308416 | tf_op jit(solution)/shard_map/reduce_scatter | solution.py:126
  934.6 56.3 %copy-start.107 = (f32[256]{0:T(256)S(1)}, f32[256]{0:T(256)}, u32[]{:S(2)}) copy-start(f32[256]{0:T(256)} %copy-done.106) | copy-start | bytes 3076
  934.7 56.9 %copy-start.7 = (f32[256,1152]{1,0:T(8,128)S(1)}, f32[256,1152]{1,0:T(8,128)}, u32[]{:S(2)}) copy-start(f32[256,1152]{1,0:T(8,128)} %get-tuple-element.58) | copy-start | bytes 3538948
  934.7 109.3 %all-gather.11.cloned.1.call-start = ((), (), s32[]{:S(2)}) async-start(), calls=%async_computation.18 | async-start | bytes 5308416 | tf_op jit(solution)/shard_map/all_gather | solution.py:122
  993.7 54.5 %copy-start.68 = (f32[8,2,256]{2,1,0:T(2,128)S(1)}, f32[8,2,256]{2,1,0:T(2,128)}, u32[]{:S(2)}) copy-start(f32[8,2,256]{2,1,0:T(2,128)} %copy-done.67) | copy-start | bytes 49156
  993.7 131.0 %reduce-scatter.23.cloned.1.call-start = ((), (), s32[]{:S(2)}) async-start(), calls=%async_computation.19 | async-start | bytes 5308416 | tf_op jit(solution)/shard_map/reduce_scatter | solution.py:126
  1060.9 332.7 %all-reduce.5.cloned.1.call-start = ((), (), s32[]{:S(2)}) async-start(), calls=%async_computation.20 | async-start | bytes 23887872 | tf_op jit(solution)/shard_map/psum | solution.py:332
  (107 other events, 903.7 us)
Sparse Core Ops, SparseCore 0:
  135.5 53.1 reduce-scatter.8
  273.9 53.0 reduce-scatter.10
  424.7 53.0 reduce-scatter.12
  479.8 73.1 all-gather.4
  607.5 56.2 reduce-scatter.16
  665.9 53.2 reduce-scatter.14
  724.8 50.0 all-gather.6
  806.6 53.7 reduce-scatter.18
  867.5 50.0 all-gather.8
  934.8 53.7 reduce-scatter.20
  993.8 50.0 all-gather.10
  1061.0 53.7 reduce-scatter.22
  1161.2 232.3 all-reduce.4
